TPU v7x, 32 devices: a whole 2x2x4 slice. The times are simulated.
32 devices in a mesh: parts: 2 (over x), grid: 8 (over z, y), depth: 2 (over core).
Axes of the slice: x: 2, y: 2, z: 4, core: 2. Of those that a mesh axis runs over, the one named last changes fastest.
Arguments:
- gate_input: bfloat16 [1024, 32768], P(('parts', 'depth'), 'grid'), parts along dimension 0, may hold values from -6 to 6
- up_input: bfloat16 [1024, 32768], P(('parts', 'depth'), 'grid'), parts along dimension 0, may hold values from -6 to 6
- code_values: bfloat16 [32768, 8192], P('grid', 'depth'), may hold values from -6 to 6, as said below
- exponents: int32 [1024, 8192], P('grid', 'depth'), may hold values from -10 to -7
- cotangent: bfloat16 [1024, 8192], P(('parts', 'depth'), 'grid'), parts along dimension 0, may hold values from -1.5 to 1.5
Outputs:
- output_rows: bfloat16 [1024, 8192], P(('parts', 'depth'), 'grid'), parts along dimension 0
- grad_gate: bfloat16 [1024, 32768], P(('parts', 'depth'), 'grid'), parts along dimension 0
- grad_up: bfloat16 [1024, 32768], P(('parts', 'depth'), 'grid'), parts along dimension 0
- grad_weight: bfloat16 [65536, 8192], P(('parts', 'grid'), 'depth'), parts along dimension 0
There are 2 independent parts, one for each index of `parts`. A program takes and returns all parts, laid end to end along the dimension named above; an argument that names none is the same for every part. Nothing has to cross between parts.
Inputs may be any that keep to these rules, and one draw needn't show every extreme that they name: `code_values`: every entry is one of the E2M1 values 0, +-0.5, +-1, +-1.5, +-2, +-3, +-4, +-6.
All inputs are finite; a program needn't handle non-finite values.
Results may differ from a plain program's by a relative error of at most 0.0049.
Values may be sent and summed in bfloat16 or wider, within the bound.
A program may use at most 448 MiB of HBM per device.

v0:
```python
import jax
import jax.numpy as jnp
from jax import lax
from jax.sharding import PartitionSpec as P


def shards(gate_input, up_input, code_values, exponents, cotangent):
    local_units = code_values.shape[0]
    scaled = jnp.exp2(exponents.astype(jnp.float32))
    blocks = code_values.astype(jnp.float32).reshape(local_units // 32, 32, -1) * scaled[:, None, :]
    weight_part = blocks.reshape(local_units, -1).astype(jnp.bfloat16)
    weight = lax.all_gather(weight_part, "depth", axis=1, tiled=True)
    gate_float = gate_input.astype(jnp.float32)
    up_float = up_input.astype(jnp.float32)
    sigmoid_gate = jax.nn.sigmoid(gate_float)
    activated = gate_float * sigmoid_gate
    hidden = (activated * up_float).astype(jnp.bfloat16)
    summed = lax.psum_scatter(
        lax.dot_general(
            weight, hidden, (((0,), (1,)), ((), ())), preferred_element_type=jnp.float32
        ),
        "grid",
        scatter_dimension=0,
        tiled=True,
    )
    output_rows = summed.T.astype(jnp.bfloat16)
    cotangent_all = lax.all_gather(cotangent, "grid", axis=1, tiled=True)
    grad_hidden = lax.dot_general(
        cotangent_all, weight, (((1,), (1,)), ((), ())), preferred_element_type=jnp.float32
    )
    slope = sigmoid_gate * (1.0 + gate_float * (1.0 - sigmoid_gate))
    grad_gate = (grad_hidden * up_float * slope).astype(jnp.bfloat16)
    grad_up = (grad_hidden * activated).astype(jnp.bfloat16)
    weight_term = lax.dot_general(
        hidden, cotangent_all, (((0,), (0,)), ((), ())), preferred_element_type=jnp.float32
    )
    grad_weight = lax.psum_scatter(weight_term, "depth", scatter_dimension=1, tiled=True).astype(
        jnp.bfloat16
    )
    return (output_rows, grad_gate, grad_up, grad_weight)


def solution(mesh):
    in_specs = (
        P(("parts", "depth"), "grid"),
        P(("parts", "depth"), "grid"),
        P("grid", "depth"),
        P("grid", "depth"),
        P(("parts", "depth"), "grid"),
    )
    out_specs = (
        P(("parts", "depth"), "grid"),
        P(("parts", "depth"), "grid"),
        P(("parts", "depth"), "grid"),
        P(("parts", "grid"), "depth"),
    )
    return jax.shard_map(shards, mesh=mesh, in_specs=in_specs, out_specs=out_specs, check_vma=False)
```

profile of v0, /device:TPU:0, one launch (start us, length us, event | category | flops | bytes accessed | tf_op | source)
XLA Modules:
  0.0 557.2 jit_solution(14383094031951518844)
XLA Ops:
  7.2 0.0 all-gather.3.cloned.1.call-start
  7.2 1.9 multiply_exponential_fusion
  9.1 23.3 %fusion = bf16[4096,4096]{1,0:T(8,128)(2,1)} fusion(bf16[4096,4096]{1,0:T(8,128)(2,1)} %param.7, f32[128,4096]{1,0:T(8,128)S(1)} %multiply_exponential_fusion), kind=kLoop, calls=%fused_computation.1 | loop fusion | flops 50331648 | bytes 69206016 | tf_op jit(solution)/shard_map/convert_element_type | solution.py:11
  32.3 0.0 all-gather.3.cloned.1.call-update
  32.4 0.0 all-gather.5.cloned.1.call-start
  32.4 0.7 all-gather.5.cloned.1.call-update
  33.1 0.0 reduce-scatter.3.cloned.1.call-start
  33.2 3.3 copy.9
  36.5 4.1 copy.10
  40.5 89.8 %all-gather.3.cloned.1.call-done = bf16[4096,8192]{1,0:T(8,128)(2,1)} async-done(((bf16[4096,4096]{1,0:T(8,128)(2,1)}), bf16[4096,8192]{1,0:T(8,128)(2,1)}) %all-gather.3.cloned.1.call-update) | async-done | bytes 67108880 | tf_op jit(solution)/shard_map/all_gather | solution.py:12
  130.3 30.2 %fusion.11 = f32[8192,256]{1,0:T(8,128)} fusion(bf16[4096,8192]{1,0:T(8,128)(2,1)} %all-gather.3.cloned.1.call-done, bf16[256,4096]{0,1:T(8,128)(2,1)} %copy.10, bf16[256,4096]{0,1:T(8,128)(2,1)S(1)} %copy.9), kind=kOutput, calls=%fused_computation.20 | convolution fusion | flops 17188257792 | bytes 79691776 | tf_op jit(solution)/shard_map/dot_general | solution.py:19
  160.5 0.0 reduce-scatter.3.cloned.1.call-update
  160.5 0.2 reduce-scatter.5.cloned.1.call-start
  160.8 46.3 %all-gather.5.cloned.1.call-done = bf16[256,8192]{1,0:T(8,128)(2,1)} async-done(((bf16[256,1024]{1,0:T(8,128)(2,1)}), bf16[256,8192]{1,0:T(8,128)(2,1)}) %all-gather.5.cloned.1.call-update) | async-done | bytes 4194320 | tf_op jit(solution)/shard_map/all_gather | solution.py:27
  207.1 49.9 %fusion.9 = f32[4096,8192]{1,0:T(8,128)} fusion(bf16[256,8192]{1,0:T(8,128)(2,1)} %all-gather.5.cloned.1.call-done, bf16[256,4096]{0,1:T(8,128)(2,1)} %copy.10, bf16[256,4096]{0,1:T(8,128)(2,1)S(1)} %copy.9), kind=kOutput, calls=%fused_computation.19 | convolution fusion | flops 17188257792 | bytes 142606336 | tf_op jit(solution)/shard_map/dot_general | solution.py:34
  257.0 0.0 reduce-scatter.5.cloned.1.call-update
  257.1 29.7 %multiply_convert_fusion = (bf16[256,4096]{0,1:T(8,128)(2,1)}, bf16[256,4096]{0,1:T(8,128)(2,1)}) fusion(bf16[256,4096]{0,1:T(8,128)(2,1)S(1)} %copy.9, bf16[256,4096]{0,1:T(8,128)(2,1)} %copy.10, bf16[4096,8192]{1,0:T(8,128)(2,1)} %all-gather.3.cloned.1.call-done, bf16[256,8192]{1,0:T(8,128)(2,1)} %all-gather.5.cloned.1.call-done), kind=kOutput, calls=%fused_computation.16 | convolution fusion | flops 17195597824 | bytes 79691776 | tf_op jit(solution)/shard_map/dot_general | solution.py:28
  286.7 4.3 copy.13
  291.0 2.8 copy.12
  293.9 64.7 %reduce-scatter.3.cloned.1.call-done = f32[1024,256]{1,0:T(8,128)} async-done(((f32[8192,256]{1,0:T(8,128)}), f32[1024,256]{1,0:T(8,128)}) %reduce-scatter.3.cloned.1.call-update) | async-done | bytes 1048592 | tf_op jit(solution)/shard_map/reduce_scatter | solution.py:18
  358.6 1.3 convert_bitcast_fusion
  359.8 1.0 copy.11
  360.8 157.4 %reduce-scatter.5.cloned.1.call-done = f32[4096,4096]{1,0:T(8,128)} async-done(((f32[4096,8192]{1,0:T(8,128)}), f32[4096,4096]{1,0:T(8,128)}) %reduce-scatter.5.cloned.1.call-update) | async-done | bytes 67108880 | tf_op jit(solution)/shard_map/reduce_scatter | solution.py:37
  518.3 32.4 %convert_element_type.43 = bf16[4096,4096]{1,0:T(8,128)(2,1)} convert(f32[4096,4096]{1,0:T(8,128)} %reduce-scatter.5.cloned.1.call-done) | non-fusion elementwise | flops 16777216 | bytes 100663296 | tf_op jit(solution)/shard_map/convert_element_type | solution.py:37
  (2 shorter events, 0.0 us)
Async XLA Ops:
  7.2 123.2 %all-gather.3.cloned.1.call-start = ((), (), s32[]{:S(2)}) async-start(), calls=%async_computation.2 | async-start | bytes 100663296 | tf_op jit(solution)/shard_map/all_gather | solution.py:12
  32.4 174.7 %all-gather.5.cloned.1.call-start = ((), (), s32[]{:S(2)}) async-start(), calls=%async_computation.4 | async-start | bytes 4718592 | tf_op jit(solution)/shard_map/all_gather | solution.py:27
  33.1 325.4 %reduce-scatter.3.cloned.1.call-start = ((), (), s32[]{:S(2)}) async-start(), calls=%async_computation.3 | async-start | bytes 9437184 | tf_op jit(solution)/shard_map/reduce_scatter | solution.py:18
  160.5 357.7 %reduce-scatter.5.cloned.1.call-start = ((), (), s32[]{:S(2)}) async-start(), calls=%async_computation.5 | async-start | bytes 201326592 | tf_op jit(solution)/shard_map/reduce_scatter | solution.py:37
  286.7 4.3 copy-start
Sparse Core Ops, SparseCore 0:
  32.5 97.7 all-gather.2
  132.5 74.5 all-gather.4
  211.3 147.2 reduce-scatter.2
  360.8 157.4 reduce-scatter.4
where the time goes:
time: 558 us; the launch traced here: 557 us
  waiting for transfers between devices  359 us (64%)
  matrix products  110 us (20%)
  other arithmetic  58.8 us (11%)
  local copies, waits for them, and re-layouts  15.5 us (3%)
  between operations  13.8 us (2%)
    reduce_scatter x1, waiting for transfers between devices, shards(): lax.psum_scatter(weight_term, 'depth', scatter_dimension=1, tiled=True)  157 us
    all_gather x1, waiting for transfers between devices, shards(): weight = lax.all_gather(weight_part, 'depth', axis=1, tiled=True)  89.8 us
    reduce_scatter x1, waiting for transfers between devices, shards(): lax.psum_scatter(lax.dot_general(weight, hidden, (((0,), (1,)), ((), ()))...  64.7 us
    dot_general x1, matrix products, shards(): lax.dot_general(hidden, cotangent_all, (((0,), (0,)), ((), ())), preferre...  49.9 us
    all_gather x1, waiting for transfers between devices, shards(): cotangent_all = lax.all_gather(cotangent, 'grid', axis=1, tiled=True)  46.3 us
    convert_element_type x1, other arithmetic, shards(): lax.psum_scatter(weight_term, 'depth', scatter_dimension=1, tiled=True)  32.4 us
    dot_general x1, matrix products, shards(): lax.dot_general(weight, hidden, (((0,), (1,)), ((), ())), preferred_eleme...  30.2 us
    dot_general x1, matrix products, shards(): lax.dot_general(cotangent_all, weight, (((1,), (1,)), ((), ())), preferre...  29.7 us
  transfers between devices with their start and end apart: 4, of which 4 were waited for; matrix products, arithmetic and copies ran while one was open for 23% of the time, Pallas kernels for 0%

commit v1 on v0

v1 whole, which is shorter than its diff:
```python
import functools

import jax
import jax.numpy as jnp
from jax import lax
from jax.experimental import pallas as pl
from jax.experimental.pallas import tpu as pltpu
from jax.sharding import PartitionSpec as P

VMEM_LIMIT = 60 * 1024 * 1024
F32, BF16 = jnp.float32, jnp.bfloat16


def tile(size, most):
    width = min(size, most)
    while size % width:
        width //= 2
    return width


def dequantized(codes, exponents):
    rows, columns = codes.shape
    scale = jnp.exp2(exponents.astype(F32)).astype(BF16)
    return (codes.reshape(rows // 32, 32, columns) * scale[:, None, :]).reshape(rows, columns)


def forward_body(depth, mine_ref, other_ref, codes_ref, exponents_ref, out_mine_ref, out_other_ref):
    units = codes_ref.shape[0]
    totals = [None, None]
    for start in range(0, units, depth):
        weight = dequantized(
            codes_ref[start : start + depth, :], exponents_ref[start // 32 : (start + depth) // 32, :]
        )
        for index, ref in enumerate((mine_ref, other_ref)):
            term = jnp.dot(ref[:, start : start + depth], weight, preferred_element_type=F32)
            totals[index] = term if totals[index] is None else totals[index] + term
    out_mine_ref[...] = totals[0].astype(out_mine_ref.dtype)
    out_other_ref[...] = totals[1].astype(out_other_ref.dtype)


def forward(mine, other, codes, exponents, dtype):
    tokens, units = mine.shape
    columns = codes.shape[1]
    width = tile(columns, 512)
    whole = pl.BlockSpec((tokens, units), lambda j: (0, 0), pipeline_mode=pl.Buffered(1))
    return pl.pallas_call(
        functools.partial(forward_body, tile(units, 1024)),
        grid=(columns // width,),
        in_specs=[
            whole,
            whole,
            pl.BlockSpec((units, width), lambda j: (0, j)),
            pl.BlockSpec((units // 32, width), lambda j: (0, j)),
        ],
        out_specs=[pl.BlockSpec((tokens, width), lambda j: (0, j))] * 2,
        out_shape=[jax.ShapeDtypeStruct((tokens, columns), dtype)] * 2,
        compiler_params=pltpu.CompilerParams(vmem_limit_bytes=VMEM_LIMIT),
        cost_estimate=pl.CostEstimate(
            flops=4 * tokens * units * columns, bytes_accessed=2 * units * columns, transcendentals=0
        ),
        name="forward",
    )(mine, other, codes, exponents)


def hidden_grad_body(depth, mine_ref, other_ref, codes_ref, exponents_ref, grad_mine_ref, grad_other_ref):
    columns = codes_ref.shape[1]
    totals = [None, None]
    for start in range(0, columns, depth):
        weight = dequantized(codes_ref[:, start : start + depth], exponents_ref[:, start : start + depth])
        for index, ref in enumerate((mine_ref, other_ref)):
            term = lax.dot_general(
                ref[:, start : start + depth], weight, (((1,), (1,)), ((), ())), preferred_element_type=F32
            )
            totals[index] = term if totals[index] is None else totals[index] + term
    grad_mine_ref[...] = totals[0].astype(grad_mine_ref.dtype)
    grad_other_ref[...] = totals[1].astype(grad_other_ref.dtype)


def hidden_grad(mine, other, codes, exponents):
    tokens, columns = mine.shape
    units = codes.shape[0]
    height = tile(units, 512)
    whole = pl.BlockSpec((tokens, columns), lambda i: (0, 0), pipeline_mode=pl.Buffered(1))
    return pl.pallas_call(
        functools.partial(hidden_grad_body, tile(columns, 1024)),
        grid=(units // height,),
        in_specs=[
            whole,
            whole,
            pl.BlockSpec((height, columns), lambda i: (i, 0)),
            pl.BlockSpec((height // 32, columns), lambda i: (i, 0)),
        ],
        out_specs=[pl.BlockSpec((tokens, height), lambda i: (0, i))] * 2,
        out_shape=[jax.ShapeDtypeStruct((tokens, units), F32), jax.ShapeDtypeStruct((tokens, units), BF16)],
        compiler_params=pltpu.CompilerParams(vmem_limit_bytes=VMEM_LIMIT),
        cost_estimate=pl.CostEstimate(
            flops=4 * tokens * units * columns, bytes_accessed=2 * units * columns, transcendentals=0
        ),
        name="hidden_grad",
    )(mine, other, codes, exponents)


def weight_grad_body(width, h_mine_ref, h_other_ref, c_mine_ref, c_other_ref, out_ref):
    left = [h_mine_ref[...].T, h_other_ref[...].T]
    for start in range(0, out_ref.shape[1], width):
        total = None
        for rows, ref in zip(left, (c_mine_ref, c_other_ref)):
            term = jnp.dot(rows, ref[:, start : start + width], preferred_element_type=F32)
            total = term if total is None else total + term
        out_ref[:, start : start + width] = total.astype(out_ref.dtype)


def weight_grad(h_mine, h_other, c_mine, c_other):
    tokens, units = h_mine.shape
    columns = c_mine.shape[1]
    height = tile(units, 512)
    whole = pl.BlockSpec((tokens, columns), lambda i: (0, 0), pipeline_mode=pl.Buffered(1))
    part = pl.BlockSpec((tokens, height), lambda i: (0, i))
    return pl.pallas_call(
        functools.partial(weight_grad_body, tile(columns, 1024)),
        grid=(units // height,),
        in_specs=[part, part, whole, whole],
        out_specs=pl.BlockSpec((height, columns), lambda i: (i, 0)),
        out_shape=jax.ShapeDtypeStruct((units, columns), BF16),
        compiler_params=pltpu.CompilerParams(vmem_limit_bytes=VMEM_LIMIT),
        cost_estimate=pl.CostEstimate(
            flops=4 * tokens * units * columns, bytes_accessed=2 * units * columns, transcendentals=0
        ),
        name="weight_grad",
    )(h_mine, h_other, c_mine, c_other)


def shards(gate_input, up_input, code_values, exponents, cotangent):
    core = lax.axis_index("depth")
    half = code_values.shape[1]

    def swap(value):
        return lax.ppermute(value, "depth", [(0, 1), (1, 0)])

    cotangent_all = lax.all_gather(cotangent, "grid", axis=1, tiled=True)
    gate_float = gate_input.astype(F32)
    up_float = up_input.astype(F32)
    sigmoid_gate = jax.nn.sigmoid(gate_float)
    activated = gate_float * sigmoid_gate
    hidden = (activated * up_float).astype(BF16)
    hidden_other = swap(hidden)
    out_mine, out_other = forward(hidden, hidden_other, code_values, exponents, BF16)
    out_came = swap(out_other)
    low = jnp.where(core == 0, out_mine, out_came)
    high = jnp.where(core == 0, out_came, out_mine)
    share = jnp.concatenate([low, high], axis=1).astype(F32)
    output_rows = lax.psum_scatter(share, "grid", scatter_dimension=1, tiled=True).astype(BF16)

    low, high = cotangent_all[:, :half], cotangent_all[:, half:]
    cot_mine = jnp.where(core == 0, low, high)
    cot_other = swap(jnp.where(core == 0, high, low))
    grad_mine, grad_other = hidden_grad(cot_mine, cot_other, code_values, exponents)
    grad_came = swap(grad_other)
    grad_weight = weight_grad(hidden, hidden_other, cot_mine, cot_other)
    grad_hidden = grad_mine + grad_came.astype(F32)
    slope = sigmoid_gate * (1.0 + gate_float * (1.0 - sigmoid_gate))
    grad_gate = (grad_hidden * up_float * slope).astype(BF16)
    grad_up = (grad_hidden * activated).astype(BF16)
    return (output_rows, grad_gate, grad_up, grad_weight)


def solution(mesh):
    tokens_units = P(("parts", "depth"), "grid")
    weights = P("grid", "depth")
    return jax.shard_map(
        shards,
        mesh=mesh,
        in_specs=(tokens_units, tokens_units, weights, weights, tokens_units),
        out_specs=(tokens_units, tokens_units, tokens_units, P(("parts", "grid"), "depth")),
        check_vma=False,
    )
```

time: 558 us -> 329 us (0.59)
  waiting for transfers between devices: 359 us -> 220 us
  matrix products: 110 us -> 0 us
  Pallas kernels: 0 us -> 72 us
  other arithmetic: 58.8 us -> 18.1 us
  local copies, waits for them, and re-layouts: 15.5 us -> 3.99 us
    dot_general x3 -> x0, matrix products: 110 us -> none  [the longest x1 49.9 us: shards(): lax.dot_general(hidden, cotangent_all, (((0,), (0,)), ((), ())), preferre...]
    reduce_scatter x2 -> x1, waiting for transfers between devices: 222 us -> 124 us  [shards(): lax.psum_scatter(share, 'grid', scatter_dimension=1, tiled=True)]
    all_gather x1 -> x0, waiting for transfers between devices: 89.8 us -> none  [shards(): weight = lax.all_gather(weight_part, 'depth', axis=1, tiled=True)]
    pallas_call x0 -> x3, Pallas kernels: none -> 72 us  [the longest x1 25 us: hidden_grad(): pl.pallas_call(functools.partial(hidden_grad_body, tile(columns, 1024)),...]
    convert_element_type x3, other arithmetic: 56.9 us -> 12.3 us  [the longest x1 6 us: shards(): grad_up = (grad_hidden * activated).astype(BF16)]
    all_gather x1, waiting for transfers between devices: 46.3 us -> 78.3 us  [shards(): cotangent_all = lax.all_gather(cotangent, 'grid', axis=1, tiled=True)]
    ppermute x0 -> x4, waiting for transfers between devices: none -> 16.6 us  [swap(): return lax.ppermute(value, 'depth', [(0, 1), (1, 0)])]
    unnamed x7 -> x8, local copies, waits for them, and re-layouts: 15.5 us -> 3.99 us
  transfers between devices with their start and end apart: 4 -> 6, of which waited for: 4 -> 6; matrix products, arithmetic and copies ran while one was open for 23% -> 0% of each run, Pallas kernels for 0% -> 7%
where the time goes in v1:
time: 329 us; the launch traced here: 328 us
  waiting for transfers between devices  220 us (67%)
  Pallas kernels  72 us (22%)
  other arithmetic  18.1 us (6%)
  between operations  14.1 us (4%)
  local copies, waits for them, and re-layouts  3.99 us (1%)
    reduce_scatter x1, waiting for transfers between devices, shards(): lax.psum_scatter(share, 'grid', scatter_dimension=1, tiled=True)  124 us
    all_gather x1, waiting for transfers between devices, shards(): cotangent_all = lax.all_gather(cotangent, 'grid', axis=1, tiled=True)  78.3 us
    pallas_call x1, Pallas kernels, hidden_grad(): pl.pallas_call(functools.partial(hidden_grad_body, tile(columns, 1024)),...  25 us
    pallas_call x1, Pallas kernels, weight_grad(): pl.pallas_call(functools.partial(weight_grad_body, tile(columns, 1024)),...  23.5 us
    pallas_call x1, Pallas kernels, forward(): pl.pallas_call(functools.partial(forward_body, tile(units, 1024)), grid=(...  23.5 us
    ppermute x4, waiting for transfers between devices, swap(): return lax.ppermute(value, 'depth', [(0, 1), (1, 0)])  16.6 us
  transfers between devices with their start and end apart: 6, of which 6 were waited for; matrix products, arithmetic and copies ran while one was open for 0% of the time, Pallas kernels for 7%

profile of v1, /device:TPU:0, one launch (start us, length us, event | category | flops | bytes accessed | tf_op | source)
XLA Modules:
  0.0 328.4 jit_solution(530879780788061520)
XLA Ops:
  7.2 0.0 all-gather.2.cloned.1.call-start
  7.2 0.7 all-gather.2.cloned.1.call-update
  7.9 0.0 reduce-scatter.2.cloned.1.call-start
  8.0 78.3 %all-gather.2.cloned.1.call-done = bf16[256,8192]{1,0:T(8,128)(2,1)} async-done(((bf16[256,1024]{1,0:T(8,128)(2,1)}), bf16[256,8192]{1,0:T(8,128)(2,1)}) %all-gather.2.cloned.1.call-update) | async-done | bytes 4194320 | tf_op jit(solution)/shard_map/all_gather | solution.py:140
  86.3 3.9 %broadcast_select_fusion = (bf16[256,4096]{1,0:T(8,128)(2,1)S(1)}, bf16[256,4096]{1,0:T(8,128)(2,1)}) fusion(pred[]{:T(512)S(6)} %eq.2, bf16[256,8192]{1,0:T(8,128)(2,1)} %all-gather.2.cloned.1.call-done), kind=kLoop, calls=%fused_computation.16 | loop fusion | flops 2097152 | bytes 8388609 | tf_op jit(solution)/shard_map/jit(_where)/select_n | solution.py:156
  90.2 4.2 %collective-permute-done.2.other_ref.c_other_ref = bf16[256,4096]{1,0:T(8,128)(2,1)S(1)} collective-permute-done((bf16[256,4096]{1,0:T(8,128)(2,1)S(1)}, bf16[256,4096]{1,0:T(8,128)(2,1)S(1)}, u32[]{:S(2)}, u32[]{:S(2)}) %collective-permute-start.2) | collective-permute-done | bytes 2097184 | tf_op jit(solution)/shard_map/ppermute | solution.py:138
  94.3 1.3 copy-done.2
  95.7 25.0 %hidden_grad.1 = (f32[256,4096]{1,0:T(8,128)}, bf16[256,4096]{1,0:T(8,128)(2,1)}) custom-call(bf16[256,4096]{1,0:T(8,128)(2,1)} %get-tuple-element.16.mine_ref.c_mine_ref, bf16[256,4096]{1,0:T(8,128)(2,1)} %copy-done.2, bf16[4096,4096]{1,0:T(8,128)(2,1)} %codes_ref.3, s32[128,4096]{1,0:T(8,128)} %exponents_ref.3), custom_call_target="tpu_custom_call" | custom-call | flops 17179869184 | bytes 33554432 | tf_op jit(solution)/shard_map/hidden_grad/pallas_call | solution.py:84
  120.6 0.1 collective-permute-start.3
  120.8 4.2 %collective-permute-done.3 = bf16[256,4096]{1,0:T(8,128)(2,1)S(1)} collective-permute-done((bf16[256,4096]{1,0:T(8,128)(2,1)}, bf16[256,4096]{1,0:T(8,128)(2,1)S(1)}, u32[]{:S(2)}, u32[]{:S(2)}) %collective-permute-start.3) | collective-permute-done | bytes 2097184 | tf_op jit(solution)/shard_map/ppermute | solution.py:138
  125.0 6.0 %multiply_convert_fusion = (bf16[256,4096]{1,0:T(8,128)(2,1)}, bf16[256,4096]{1,0:T(8,128)(2,1)}, bf16[256,4096]{1,0:T(8,128)(2,1)S(1)}) fusion(f32[256,4096]{1,0:T(8,128)} %get-tuple-element.10, bf16[256,4096]{1,0:T(8,128)(2,1)S(1)} %collective-permute-done.3, bf16[256,4096]{1,0:T(8,128)(2,1)S(1)} %copy-done, bf16[256,4096]{1,0:T(8,128)(2,1)} %param.6), kind=kLoop, calls=%fused_computation.14 | loop fusion | flops 19922944 | bytes 16777216 | tf_op jit(solution)/shard_map/convert_element_type | solution.py:163
  131.0 1.3 copy-done.1
  132.4 0.1 collective-permute-start
  132.5 4.0 %collective-permute-done.other_ref.h_other_ref = bf16[256,4096]{1,0:T(8,128)(2,1)S(1)} collective-permute-done((bf16[256,4096]{1,0:T(8,128)(2,1)S(1)}, bf16[256,4096]{1,0:T(8,128)(2,1)S(1)}, u32[]{:S(2)}, u32[]{:S(2)}) %collective-permute-start) | collective-permute-done | bytes 2097184 | tf_op jit(solution)/shard_map/ppermute | solution.py:138
  136.5 1.3 copy-done.3
  137.8 23.5 %forward.1 = (bf16[256,4096]{1,0:T(8,128)(2,1)}, bf16[256,4096]{1,0:T(8,128)(2,1)}) custom-call(bf16[256,4096]{1,0:T(8,128)(2,1)} %copy-done.1, bf16[256,4096]{1,0:T(8,128)(2,1)} %copy-done.3, bf16[4096,4096]{1,0:T(8,128)(2,1)} %codes_ref.3, s32[128,4096]{1,0:T(8,128)} %exponents_ref.3), custom_call_target="tpu_custom_call" | custom-call | flops 17179869184 | bytes 33554432 | tf_op jit(solution)/shard_map/forward/pallas_call | solution.py:46
  161.3 0.1 collective-permute-start.1
  161.4 4.2 %collective-permute-done.1 = bf16[256,4096]{1,0:T(8,128)(2,1)S(1)} collective-permute-done((bf16[256,4096]{1,0:T(8,128)(2,1)}, bf16[256,4096]{1,0:T(8,128)(2,1)S(1)}, u32[]{:S(2)}, u32[]{:S(2)}) %collective-permute-start.1) | collective-permute-done | bytes 2097184 | tf_op jit(solution)/shard_map/ppermute | solution.py:138
  165.7 1.9 broadcast_select_fusion.3
  167.5 4.2 %maximum_convert_fusion = f32[256,8192]{1,0:T(8,128)} fusion(bf16[256,4096]{1,0:T(8,128)(2,1)S(1)} %get-tuple-element.18, bf16[256,4096]{1,0:T(8,128)(2,1)S(1)} %get-tuple-element.17), kind=kLoop, calls=%fused_computation.13 | loop fusion | flops 8388608 | bytes 12582912 | tf_op jit(solution)/shard_map/convert_element_type | solution.py:151
  171.8 0.0 reduce-scatter.2.cloned.1.call-update
  171.8 23.5 %weight_grad.1 = bf16[4096,4096]{1,0:T(8,128)(2,1)} custom-call(bf16[256,4096]{1,0:T(8,128)(2,1)} %copy-done.1, bf16[256,4096]{1,0:T(8,128)(2,1)} %copy-done.3, bf16[256,4096]{1,0:T(8,128)(2,1)} %get-tuple-element.16.mine_ref.c_mine_ref, bf16[256,4096]{1,0:T(8,128)(2,1)} %copy-done.2), custom_call_target="tpu_custom_call" | custom-call | flops 17179869184 | bytes 33554432 | tf_op jit(solution)/shard_map/weight_grad/pallas_call | solution.py:119
  195.3 124.2 %reduce-scatter.2.cloned.1.call-done = f32[256,1024]{1,0:T(8,128)} async-done(((f32[256,8192]{1,0:T(8,128)}), f32[256,1024]{1,0:T(8,128)}) %reduce-scatter.2.cloned.1.call-update) | async-done | bytes 1048592 | tf_op jit(solution)/shard_map/reduce_scatter | solution.py:152
  319.5 2.1 convert_element_type.28
  (6 shorter events, 0.0 us)
Async XLA Ops:
  7.2 79.1 %all-gather.2.cloned.1.call-start = ((), (), s32[]{:S(2)}) async-start(), calls=%async_computation.2 | async-start | bytes 4718592 | tf_op jit(solution)/shard_map/all_gather | solution.py:140
  7.9 311.6 %reduce-scatter.2.cloned.1.call-start = ((), (), s32[]{:S(2)}) async-start(), calls=%async_computation.1 | async-start | bytes 9437184 | tf_op jit(solution)/shard_map/reduce_scatter | solution.py:152
  90.2 4.2 %collective-permute-start.2 = (bf16[256,4096]{1,0:T(8,128)(2,1)S(1)}, bf16[256,4096]{1,0:T(8,128)(2,1)S(1)}, u32[]{:S(2)}, u32[]{:S(2)}) collective-permute-start(bf16[256,4096]{1,0:T(8,128)(2,1)S(1)} %get-tuple-element.15), channel_id=1, source_target_pairs={{0,1},{1,0},{2,3},{3,2},{4,5},{5,4},{6,7},{7,6},{8,9},{9,8},{10,11... | collective-permute-start | bytes 6291464 | tf_op jit(solution)/shard_map/ppermute | solution.py:138
  94.3 1.3 copy-start.2
  95.7 29.4 %copy-start = (bf16[256,4096]{1,0:T(8,128)(2,1)S(1)}, bf16[256,4096]{1,0:T(8,128)(2,1)}, u32[]{:S(2)}) copy-start(bf16[256,4096]{1,0:T(8,128)(2,1)} %param.5) | copy-start | bytes 6291460
  120.6 4.4 %collective-permute-start.3 = (bf16[256,4096]{1,0:T(8,128)(2,1)}, bf16[256,4096]{1,0:T(8,128)(2,1)S(1)}, u32[]{:S(2)}, u32[]{:S(2)}) collective-permute-start(bf16[256,4096]{1,0:T(8,128)(2,1)} %get-tuple-element.11), channel_id=1, source_target_pairs={{0,1},{1,0},{2,3},{3,2},{4,5},{5,4},{6,7},{7,6},{8,9},{9,8},{10,11... | collective-permute-start | bytes 6291464 | tf_op jit(solution)/shard_map/ppermute | solution.py:138
  131.0 1.3 copy-start.1
  132.4 4.2 %collective-permute-start = (bf16[256,4096]{1,0:T(8,128)(2,1)S(1)}, bf16[256,4096]{1,0:T(8,128)(2,1)S(1)}, u32[]{:S(2)}, u32[]{:S(2)}) collective-permute-start(bf16[256,4096]{1,0:T(8,128)(2,1)S(1)} %get-tuple-element.14.mine_ref.h_mine_ref), channel_id=1, source_target_pairs={{0,1},{1,0},{2,3},{3,2},{4,5},{5,4},{6,7},{7,6},{8,9},{9,8},{10,11... | collective-permute-start | bytes 6291464 | tf_op jit(solution)/shard_map/ppermute | solution.py:138
  136.5 1.3 copy-start.3
  161.3 4.4 %collective-permute-start.1 = (bf16[256,4096]{1,0:T(8,128)(2,1)}, bf16[256,4096]{1,0:T(8,128)(2,1)S(1)}, u32[]{:S(2)}, u32[]{:S(2)}) collective-permute-start(bf16[256,4096]{1,0:T(8,128)(2,1)} %get-tuple-element.9), channel_id=1, source_target_pairs={{0,1},{1,0},{2,3},{3,2},{4,5},{5,4},{6,7},{7,6},{8,9},{9,8},{10,11... | collective-permute-start | bytes 6291464 | tf_op jit(solution)/shard_map/ppermute | solution.py:138
Sparse Core Ops, SparseCore 0:
  10.2 76.0 all-gather.1
  171.9 147.5 reduce-scatter.1

commit v2 on v1

v2 whole, which is shorter than its diff:
```python
import functools

import jax
import jax.numpy as jnp
from jax import lax
from jax.experimental import pallas as pl
from jax.experimental.pallas import tpu as pltpu
from jax.sharding import PartitionSpec as P

VMEM_LIMIT = 60 * 1024 * 1024
F32, BF16 = jnp.float32, jnp.bfloat16


MESH = pl.DeviceIdType.MESH


def line_sizes(count):
    fast = 1
    while 4 * fast * fast <= count:
        fast *= 2
    return count // fast, fast


def position(fast):
    me = lax.axis_index("grid")
    return me, me // fast, me % fast, lax.axis_index("depth")


def greet(slow, fast):
    me, row, column, core = position(fast)
    barrier = pltpu.get_barrier_semaphore()

    def hail(grid, depth):
        pl.semaphore_signal(barrier, inc=1, device_id={"grid": grid, "depth": depth}, device_id_type=MESH)

    for step in range(1, slow):
        hail((row + step) % slow * fast + column, core)
    for step in range(1, fast):
        for depth in range(2):
            hail(row * fast + (column + step) % fast, depth)
    hail(me, 1 - core)
    pl.semaphore_wait(barrier, slow - 1 + 2 * (fast - 1) + 1)


def remote(source, target, send, recv, grid, depth):
    return pltpu.make_async_remote_copy(
        src_ref=source,
        dst_ref=target,
        send_sem=send,
        recv_sem=recv,
        device_id={"grid": grid, "depth": depth},
        device_id_type=MESH,
    )


def tile(size, most):
    width = min(size, most)
    while size % width:
        width //= 2
    return width


def dequantized(codes, exponents):
    rows, columns = codes.shape
    scale = jnp.exp2(exponents.astype(F32)).astype(BF16)
    return (codes.reshape(rows // 32, 32, columns) * scale[:, None, :]).reshape(rows, columns)


def forward_body(
    depth,
    slow,
    fast,
    mine_ref,
    other_ref,
    codes_ref,
    exponents_ref,
    cot_ref,
    out_mine_ref,
    out_other_ref,
    all_ref,
    own_sem,
    line_sem,
    relay_sem,
    recv_sem,
):
    step = pl.program_id(0)
    last = pl.num_programs(0) - 1
    me, row, column, core = position(fast)
    width = cot_ref.shape[1]
    near = slow // 2

    def away(source_row):
        gap = source_row // near - core
        return gap * gap

    def piece(section, source_row, source_column):
        index = source_row % near * fast + source_column
        place = all_ref.at[section, :, pl.ds(pl.multiple_of(index * width, width), width)]
        return place, recv_sem.at[section, index]

    own_place, own_recv = piece(2 * away(row), row, column)

    def keep_own():
        return pltpu.make_async_copy(cot_ref, own_place, own_sem)

    def along(hop):
        return remote(
            cot_ref, own_place, line_sem.at[hop], own_recv, (row + hop) % slow * fast + column, core
        )

    def across(hop, turn):
        source_row = (row + hop) % slow
        source = cot_ref if hop == 0 else piece(2 * away(source_row), source_row, column)[0]
        place, recv = piece(away(source_row), source_row, column)
        target = row * fast + (column + turn) % fast
        return remote(source, place, relay_sem.at[hop, turn], recv, target, source_row // near)

    def relay(hop, finish):
        def one(turn):
            copy = across(hop, turn)
            if finish:
                copy.wait_send()
            else:
                copy.start()

        for turn in range(1, fast):
            one(turn)

        @pl.when(away((row + hop) % slow) == 1)
        def _():
            one(0)

    def arrive(section, source_row, source_column):
        place, recv = piece(section, source_row, source_column)
        pltpu.make_async_copy(place, place, recv).wait()

    @pl.when(step == 0)
    def _():
        greet(slow, fast)
        for hop in range(1, slow):
            along(hop).start()
        relay(0, False)

        @pl.when(away(row) == 0)
        def _():
            keep_own().start()

    units = codes_ref.shape[0]
    totals = [None, None]
    for start in range(0, units, depth):
        weight = dequantized(
            codes_ref[start : start + depth, :], exponents_ref[start // 32 : (start + depth) // 32, :]
        )
        for index, ref in enumerate((mine_ref, other_ref)):
            term = jnp.dot(ref[:, start : start + depth], weight, preferred_element_type=F32)
            totals[index] = term if totals[index] is None else totals[index] + term
    out_mine_ref[...] = totals[0].astype(out_mine_ref.dtype)
    out_other_ref[...] = totals[1].astype(out_other_ref.dtype)

    for count, hop in enumerate(range(1, slow)):

        @pl.when(step == jnp.minimum(last, (count + 1) * (last + 1) // (slow - 1)))
        def _():
            source_row = (row + hop) % slow
            arrive(2 * away(source_row), source_row, column)
            relay(hop, False)

    @pl.when(step == last)
    def _():
        for index in range(near):
            for turn in range(1, fast):
                arrive(0, core * near + index, (column + turn) % fast)
            for source_column in range(fast):
                arrive(1, core * near + index, source_column)
        for hop in range(1, slow):
            along(hop).wait_send()
        for hop in range(slow):
            relay(hop, True)

        @pl.when(away(row) == 0)
        def _():
            keep_own().wait()


def forward(mine, other, codes, exponents, cotangent, slow, fast):
    tokens, units = mine.shape
    columns = codes.shape[1]
    width = tile(columns, 512)
    whole = pl.BlockSpec((tokens, units), lambda j: (0, 0), pipeline_mode=pl.Buffered(1))
    anywhere = pl.BlockSpec(memory_space=pl.ANY)
    dma = pltpu.SemaphoreType.DMA
    return pl.pallas_call(
        functools.partial(forward_body, tile(units, 1024), slow, fast),
        grid=(columns // width,),
        in_specs=[
            whole,
            whole,
            pl.BlockSpec((units, width), lambda j: (0, j)),
            pl.BlockSpec((units // 32, width), lambda j: (0, j)),
            anywhere,
        ],
        out_specs=[pl.BlockSpec((tokens, width), lambda j: (0, j))] * 2 + [anywhere],
        out_shape=[jax.ShapeDtypeStruct((tokens, columns), BF16)] * 2
        + [jax.ShapeDtypeStruct((3, tokens, columns), BF16)],
        scratch_shapes=[dma, dma((slow,)), dma((slow, fast)), dma((3, slow * fast // 2))],
        compiler_params=pltpu.CompilerParams(
            vmem_limit_bytes=VMEM_LIMIT, collective_id=0, has_side_effects=True
        ),
        cost_estimate=pl.CostEstimate(
            flops=4 * tokens * units * columns, bytes_accessed=2 * units * columns, transcendentals=0
        ),
        name="forward",
    )(mine, other, codes, exponents, cotangent)


def hidden_grad_body(
    depth,
    slow,
    fast,
    mine_ref,
    other_ref,
    codes_ref,
    exponents_ref,
    out_mine_ref,
    out_other_ref,
    grad_mine_ref,
    grad_other_ref,
    rows_ref,
    first_ref,
    sums_ref,
    second_ref,
    first_send,
    first_recv,
    second_send,
    second_recv,
):
    step = pl.program_id(0)
    last = pl.num_programs(0) - 1
    me, row, column, core = position(fast)
    width = rows_ref.shape[1]
    near = slow // 2

    def block(ref, index, turn):
        start = (index * fast + (column + turn) % fast) * width
        return ref.at[:, pl.ds(pl.multiple_of(start, width), width)]

    def keep_own(index):
        target_row = core * near + index
        return pltpu.make_async_copy(
            block(out_mine_ref, index, 0), first_ref.at[target_row, column], first_recv.at[target_row, column]
        )

    def across(index, turn, other):
        target_row = core * near + index
        return remote(
            block(out_other_ref if other else out_mine_ref, index, turn),
            first_ref.at[target_row, column],
            first_send.at[index, turn, other],
            first_recv.at[target_row, column],
            row * fast + (column + turn) % fast,
            1 - core if other else core,
        )

    def crossings():
        return [
            (index, turn, other)
            for index in range(near)
            for turn in [*range(1, fast), 0]
            for other in range(2)
            if turn or other
        ]

    def gathered(target_row):
        total = None
        for source in range(fast):
            place = first_ref.at[target_row, source]
            pltpu.make_async_copy(place, place, first_recv.at[target_row, source]).wait()
            term = first_ref[target_row, source].astype(F32)
            total = term if total is None else total + term
        return total

    def along(hop):
        target_row = (row + hop) % slow
        return remote(
            sums_ref.at[hop],
            second_ref.at[row],
            second_send.at[hop],
            second_recv.at[row],
            target_row * fast + column,
            core,
        )

    @pl.when(step == 0)
    def _():
        greet(slow, fast)
        for crossing in crossings():
            across(*crossing).start()
        for index in range(near):
            keep_own(index).start()

    columns = codes_ref.shape[1]
    totals = [None, None]
    for start in range(0, columns, depth):
        weight = dequantized(codes_ref[:, start : start + depth], exponents_ref[:, start : start + depth])
        for index, ref in enumerate((mine_ref, other_ref)):
            term = lax.dot_general(
                ref[:, start : start + depth], weight, (((1,), (1,)), ((), ())), preferred_element_type=F32
            )
            totals[index] = term if totals[index] is None else totals[index] + term
    grad_mine_ref[...] = totals[0].astype(grad_mine_ref.dtype)
    grad_other_ref[...] = totals[1].astype(grad_other_ref.dtype)

    for hop in range(1, slow):

        @pl.when(step == jnp.minimum(last, hop * (last + 1) // (slow - 1)))
        def _():
            sums_ref[hop] = gathered((row + hop) % slow).astype(BF16)
            along(hop).start()

    @pl.when(step == last)
    def _():
        total = gathered(row)
        for hop in range(1, slow):
            source = (row + hop) % slow
            place = second_ref.at[source]
            pltpu.make_async_copy(place, place, second_recv.at[source]).wait()
            total = total + second_ref[source].astype(F32)
        rows_ref[...] = total.astype(rows_ref.dtype)
        for crossing in crossings():
            across(*crossing).wait_send()
        for hop in range(1, slow):
            along(hop).wait_send()


def hidden_grad(cot_all, codes, exponents, out_mine, out_other, slow, fast):
    _, tokens, columns = cot_all.shape
    units = codes.shape[0]
    height = tile(units, 512)
    width = columns * 2 // (slow * fast)
    anywhere = pl.BlockSpec(memory_space=pl.ANY)
    dma = pltpu.SemaphoreType.DMA
    return pl.pallas_call(
        functools.partial(hidden_grad_body, tile(columns, 1024), slow, fast),
        grid=(units // height,),
        in_specs=[
            pl.BlockSpec((None, tokens, columns), lambda i: (0, 0, 0), pipeline_mode=pl.Buffered(1)),
            pl.BlockSpec((None, tokens, columns), lambda i: (1, 0, 0), pipeline_mode=pl.Buffered(1)),
            pl.BlockSpec((height, columns), lambda i: (i, 0)),
            pl.BlockSpec((height // 32, columns), lambda i: (i, 0)),
            anywhere,
            anywhere,
        ],
        out_specs=[pl.BlockSpec((tokens, height), lambda i: (0, i))] * 2
        + [pl.BlockSpec((tokens, width), lambda i: (0, 0))],
        out_shape=[
            jax.ShapeDtypeStruct((tokens, units), F32),
            jax.ShapeDtypeStruct((tokens, units), BF16),
            jax.ShapeDtypeStruct((tokens, width), BF16),
        ],
        scratch_shapes=[
            pltpu.VMEM((slow, fast, tokens, width), BF16),
            pltpu.VMEM((slow, tokens, width), BF16),
            pltpu.VMEM((slow, tokens, width), BF16),
            dma((slow // 2, fast, 2)),
            dma((slow, fast)),
            dma((slow,)),
            dma((slow,)),
        ],
        compiler_params=pltpu.CompilerParams(
            vmem_limit_bytes=VMEM_LIMIT, collective_id=1, has_side_effects=True
        ),
        cost_estimate=pl.CostEstimate(
            flops=4 * tokens * units * columns, bytes_accessed=2 * units * columns, transcendentals=0
        ),
        name="hidden_grad",
    )(cot_all, cot_all, codes, exponents, out_mine, out_other)


def weight_grad_body(width, h_mine_ref, h_other_ref, c_mine_ref, c_other_ref, out_ref):
    left = [h_mine_ref[...].T, h_other_ref[...].T]
    for start in range(0, out_ref.shape[1], width):
        total = None
        for rows, ref in zip(left, (c_mine_ref, c_other_ref)):
            term = jnp.dot(rows, ref[:, start : start + width], preferred_element_type=F32)
            total = term if total is None else total + term
        out_ref[:, start : start + width] = total.astype(out_ref.dtype)


def weight_grad(h_mine, h_other, cot_all):
    tokens, units = h_mine.shape
    columns = cot_all.shape[2]
    height = tile(units, 512)
    first = pl.BlockSpec((None, tokens, columns), lambda i: (0, 0, 0), pipeline_mode=pl.Buffered(1))
    second = pl.BlockSpec((None, tokens, columns), lambda i: (1, 0, 0), pipeline_mode=pl.Buffered(1))
    part = pl.BlockSpec((tokens, height), lambda i: (0, i))
    return pl.pallas_call(
        functools.partial(weight_grad_body, tile(columns, 1024)),
        grid=(units // height,),
        in_specs=[part, part, first, second],
        out_specs=pl.BlockSpec((height, columns), lambda i: (i, 0)),
        out_shape=jax.ShapeDtypeStruct((units, columns), BF16),
        compiler_params=pltpu.CompilerParams(vmem_limit_bytes=VMEM_LIMIT),
        cost_estimate=pl.CostEstimate(
            flops=4 * tokens * units * columns, bytes_accessed=2 * units * columns, transcendentals=0
        ),
        name="weight_grad",
    )(h_mine, h_other, cot_all, cot_all)


def shards(slow, fast, gate_input, up_input, code_values, exponents, cotangent):
    def swap(value):
        return lax.ppermute(value, "depth", [(0, 1), (1, 0)])

    gate_float = gate_input.astype(F32)
    up_float = up_input.astype(F32)
    sigmoid_gate = jax.nn.sigmoid(gate_float)
    activated = gate_float * sigmoid_gate
    hidden = (activated * up_float).astype(BF16)
    hidden_other = swap(hidden)
    out_mine, out_other, cot_all = forward(
        hidden, hidden_other, code_values, exponents, cotangent, slow, fast
    )
    grad_mine, grad_other, output_rows = hidden_grad(
        cot_all, code_values, exponents, out_mine, out_other, slow, fast
    )
    grad_came = swap(grad_other)
    grad_weight = weight_grad(hidden, hidden_other, cot_all)
    grad_hidden = grad_mine + grad_came.astype(F32)
    slope = sigmoid_gate * (1.0 + gate_float * (1.0 - sigmoid_gate))
    grad_gate = (grad_hidden * up_float * slope).astype(BF16)
    grad_up = (grad_hidden * activated).astype(BF16)
    return (output_rows, grad_gate, grad_up, grad_weight)


def solution(mesh):
    tokens_units = P(("parts", "depth"), "grid")
    weights = P("grid", "depth")
    slow, fast = line_sizes(mesh.shape["grid"])
    return jax.shard_map(
        functools.partial(shards, slow, fast),
        mesh=mesh,
        in_specs=(tokens_units, tokens_units, weights, weights, tokens_units),
        out_specs=(tokens_units, tokens_units, tokens_units, P(("parts", "grid"), "depth")),
        check_vma=False,
    )
```

time: 329 us -> 212 us (0.64)
  waiting for transfers between devices: 220 us -> 3.92 us
  Pallas kernels: 72 us -> 189 us
  between operations: 14.1 us -> 0.67 us
  other arithmetic: 18.1 us -> 9.5 us
  starting transfers between devices: 0.49 us -> 6.25 us
    reduce_scatter x1 -> x0, waiting for transfers between devices: 124 us -> none  [shards(): lax.psum_scatter(share, 'grid', scatter_dimension=1, tiled=True)]
    pallas_call x2, Pallas kernels: 48.4 us -> 165 us  [the longest x1 96.2 us: hidden_grad(): pl.pallas_call(functools.partial(hidden_grad_body, tile(columns, 1024), s...]
    all_gather x1 -> x0, waiting for transfers between devices: 78.3 us -> none  [shards(): cotangent_all = lax.all_gather(cotangent, 'grid', axis=1, tiled=True)]
    ppermute x4 -> x2, waiting for transfers between devices: 16.6 us -> 3.92 us  [swap(): return lax.ppermute(value, 'depth', [(0, 1), (1, 0)])]
    ppermute x4 -> x2, starting transfers between devices: 0.41 us -> 6.25 us  [swap(): return lax.ppermute(value, 'depth', [(0, 1), (1, 0)])]
    select_n x2 -> x0, other arithmetic: 5.73 us -> none  [the longest x1 3.86 us: shards(): cot_other = swap(jnp.where(core == 0, high, low))]
  transfers between devices with their start and end apart: 6 -> 2, of which waited for: 6 -> 1; matrix products, arithmetic and copies ran while one was open for 0% -> 0% of each run, Pallas kernels for 7% -> 11%
where the time goes in v2:
time: 212 us; the launch traced here: 210 us
  Pallas kernels  189 us (89%)
  other arithmetic  9.5 us (4%)
  starting transfers between devices  6.25 us (3%)
  waiting for transfers between devices  3.92 us (2%)
    pallas_call x1, Pallas kernels, hidden_grad(): pl.pallas_call(functools.partial(hidden_grad_body, tile(columns, 1024), s...  96.2 us
    pallas_call x1, Pallas kernels, forward(): pl.pallas_call(functools.partial(forward_body, tile(units, 1024), slow, f...  69.1 us
    pallas_call x1, Pallas kernels, weight_grad(): pl.pallas_call(functools.partial(weight_grad_body, tile(columns, 1024)),...  23.6 us
    ppermute x2, starting transfers between devices, swap(): return lax.ppermute(value, 'depth', [(0, 1), (1, 0)])  6.25 us
    convert_element_type x1, other arithmetic, shards(): grad_up = (grad_hidden * activated).astype(BF16)  5.95 us
  transfers between devices with their start and end apart: 2, of which 1 were waited for; matrix products, arithmetic and copies ran while one was open for 0% of the time, Pallas kernels for 11%

profile of v2, /device:TPU:0, one launch (start us, length us, event | category | flops | bytes accessed | tf_op | source)
XLA Modules:
  0.0 210.1 jit_solution(5584746646269846438)
XLA Ops:
  0.6 3.6 %fusion.mine_ref.h_mine_ref = bf16[256,4096]{1,0:T(8,128)(2,1)S(1)} fusion(bf16[256,4096]{1,0:T(8,128)(2,1)} %param.6, bf16[256,4096]{1,0:T(8,128)(2,1)} %param.5), kind=kLoop, calls=%fused_computation.5 | loop fusion | flops 8388608 | bytes 6291456 | tf_op jit(solution)/shard_map/convert_element_type | solution.py:418
  4.2 0.0 copy-start.1
  4.2 0.5 collective-permute-start
  4.7 3.9 %collective-permute-done.other_ref.h_other_ref = bf16[256,4096]{1,0:T(8,128)(2,1)} collective-permute-done((bf16[256,4096]{1,0:T(8,128)(2,1)S(1)}, bf16[256,4096]{1,0:T(8,128)(2,1)}, u32[]{:S(2)}, u32[]{:S(2)}) %collective-permute-start) | collective-permute-done | bytes 2097184 | tf_op jit(solution)/shard_map/ppermute | solution.py:412
  8.6 0.0 copy-done.1
  8.6 69.1 %forward.1 = (bf16[256,4096]{1,0:T(8,128)(2,1)}, bf16[256,4096]{1,0:T(8,128)(2,1)}, bf16[3,256,4096]{2,1,0:T(8,128)(2,1)}) custom-call(bf16[256,4096]{1,0:T(8,128)(2,1)} %copy-done.1, bf16[256,4096]{1,0:T(8,128)(2,1)} %collective-permute-done.other_ref.h_other_ref, bf16[4096,4096]{1,0:T(8,128)(2,1)} %codes_ref.3, s32[128,4096]{1,0:T(8,128)} %exponents_ref.3, ...), custom_call_target="tpu_custom_call" | custom-call | flops 17179869184 | bytes 33554432 | tf_op jit(solution)/shard_map/forward/pallas_call | solution.py:192
  77.7 96.2 %hidden_grad.1 = (f32[256,4096]{1,0:T(8,128)}, bf16[256,4096]{1,0:T(8,128)(2,1)}, bf16[256,1024]{1,0:T(8,128)(2,1)}) custom-call(bf16[3,256,4096]{2,1,0:T(8,128)(2,1)} %get-tuple-element.10.mine_ref.other_ref.c_mine_ref.c_other_ref, bf16[3,256,4096]{2,1,0:T(8,128)(2,1)} %get-tuple-element.10.mine_ref.other_ref.c_mine_ref.c_other_ref, ...), custom_call_target="tpu_custom_call" | custom-call | flops 17179869184 | bytes 33554432 | tf_op jit(solution)/shard_map/hidden_grad/pallas_call | solution.py:342
  174.0 5.7 %collective-permute-start.1 = (bf16[256,4096]{1,0:T(8,128)(2,1)}, bf16[256,4096]{1,0:T(8,128)(2,1)}, u32[]{:S(2)}, u32[]{:S(2)}) collective-permute-start(bf16[256,4096]{1,0:T(8,128)(2,1)} %get-tuple-element.15), channel_id=1, source_target_pairs={{0,1},{1,0},{2,3},{3,2},{4,5},{5,4},{6,7},{7,6},{8,9},{9,8},{10,11... | collective-permute-start | bytes 6291464 | tf_op jit(solution)/shard_map/ppermute | solution.py:412
  179.7 0.0 copy-start
  179.7 23.6 %weight_grad.1 = bf16[4096,4096]{1,0:T(8,128)(2,1)} custom-call(bf16[256,4096]{1,0:T(8,128)(2,1)} %copy-done.1, bf16[256,4096]{1,0:T(8,128)(2,1)} %collective-permute-done.other_ref.h_other_ref, bf16[3,256,4096]{2,1,0:T(8,128)(2,1)} %get-tuple-element.10.mine_ref.other_ref.c_mine_ref.c_other_ref, ...), custom_call_target="tpu_custom_call" | custom-call | flops 17179869184 | bytes 33554432 | tf_op jit(solution)/shard_map/weight_grad/pallas_call | solution.py:396
  203.3 0.0 collective-permute-done.1
  203.3 0.0 copy-done
  203.3 0.0 copy-start.2
  203.4 5.9 %multiply_convert_fusion = (bf16[256,4096]{1,0:T(8,128)(2,1)}, bf16[256,4096]{1,0:T(8,128)(2,1)}) fusion(f32[256,4096]{1,0:T(8,128)} %get-tuple-element.14, bf16[256,4096]{1,0:T(8,128)(2,1)} %collective-permute-done.1, bf16[256,4096]{1,0:T(8,128)(2,1)} %param.5, bf16[256,4096]{1,0:T(8,128)(2,1)S(1)} %copy-done), kind=kLoop, calls=%fused_computation.13 | loop fusion | flops 17825792 | bytes 14680064 | tf_op jit(solution)/shard_map/convert_element_type | solution.py:431
  209.3 0.0 copy-done.2
  209.3 0.8 copy.10
Async XLA Ops:
  4.2 4.5 %copy-start.1 = (bf16[256,4096]{1,0:T(8,128)(2,1)}, bf16[256,4096]{1,0:T(8,128)(2,1)S(1)}, u32[]{:S(2)}) copy-start(bf16[256,4096]{1,0:T(8,128)(2,1)S(1)} %fusion.mine_ref.h_mine_ref) | copy-start | bytes 6291460
  4.2 4.4 %collective-permute-start = (bf16[256,4096]{1,0:T(8,128)(2,1)S(1)}, bf16[256,4096]{1,0:T(8,128)(2,1)}, u32[]{:S(2)}, u32[]{:S(2)}) collective-permute-start(bf16[256,4096]{1,0:T(8,128)(2,1)S(1)} %fusion.mine_ref.h_mine_ref), channel_id=1, source_target_pairs={{0,1},{1,0},{2,3},{3,2},{4,5},{5,4},{6,7},{7,6},{8,9},{9,8},{10,11... | collective-permute-start | bytes 6291464 | tf_op jit(solution)/shard_map/ppermute | solution.py:412
  174.0 29.4 %collective-permute-start.1 = (bf16[256,4096]{1,0:T(8,128)(2,1)}, bf16[256,4096]{1,0:T(8,128)(2,1)}, u32[]{:S(2)}, u32[]{:S(2)}) collective-permute-start(bf16[256,4096]{1,0:T(8,128)(2,1)} %get-tuple-element.15), channel_id=1, source_target_pairs={{0,1},{1,0},{2,3},{3,2},{4,5},{5,4},{6,7},{7,6},{8,9},{9,8},{10,11... | collective-permute-start | bytes 6291464 | tf_op jit(solution)/shard_map/ppermute | solution.py:412
  179.7 23.6 %copy-start = (bf16[256,4096]{1,0:T(8,128)(2,1)S(1)}, bf16[256,4096]{1,0:T(8,128)(2,1)}, u32[]{:S(2)}) copy-start(bf16[256,4096]{1,0:T(8,128)(2,1)} %param.6) | copy-start | bytes 6291460
  203.3 6.0 %copy-start.2 = (bf16[256,1024]{1,0:T(8,128)(2,1)S(1)}, bf16[256,1024]{1,0:T(8,128)(2,1)}, u32[]{:S(2)}) copy-start(bf16[256,1024]{1,0:T(8,128)(2,1)} %get-tuple-element.22) | copy-start | bytes 1572868

commit v3 on v2

--- a/solution.py
+++ b/solution.py
@@ -98,6 +98,7 @@
         place = all_ref.at[section, :, pl.ds(pl.multiple_of(index * width, width), width)]
         return place, recv_sem.at[section, index]
 
+    order = sorted(range(1, slow), key=lambda hop: hop * (slow - hop))
     own_place, own_recv = piece(2 * away(row), row, column)
 
     def keep_own():
@@ -137,8 +138,7 @@
     @pl.when(step == 0)
     def _():
         greet(slow, fast)
-        for hop in range(1, slow):
-            along(hop).start()
+        along(order[0]).start()
         relay(0, False)
 
         @pl.when(away(row) == 0)
@@ -157,12 +157,14 @@
     out_mine_ref[...] = totals[0].astype(out_mine_ref.dtype)
     out_other_ref[...] = totals[1].astype(out_other_ref.dtype)
 
-    for count, hop in enumerate(range(1, slow)):
+    for count, hop in enumerate(slow - hop for hop in order):
 
         @pl.when(step == jnp.minimum(last, (count + 1) * (last + 1) // (slow - 1)))
         def _():
             source_row = (row + hop) % slow
             arrive(2 * away(source_row), source_row, column)
+            if count + 1 < len(order):
+                along(order[count + 1]).start()
             relay(hop, False)
 
     @pl.when(step == last)
@@ -261,14 +263,20 @@
             1 - core if other else core,
         )
 
-    def crossings():
-        return [
-            (index, turn, other)
-            for index in range(near)
-            for turn in [*range(1, fast), 0]
-            for other in range(2)
-            if turn or other
-        ]
+    def crossings(wave):
+        index = (row + 1 + wave) % near
+        turns = [*range(1, fast), 0]
+        return [across(index, turn, other) for turn in turns for other in range(2) if turn or other]
+
+    def launch(wave):
+        for copy in crossings(wave):
+            copy.start()
+        keep_own((row + 1 + wave) % near).start()
+
+    def targets(wave):
+        index = (row + 1 + wave) % near
+        distant = (row // near + 1) % 2 * near + index
+        return [distant] if wave == near - 1 else [distant, row // near * near + index]
 
     def gathered(target_row):
         total = None
@@ -279,12 +287,11 @@
             total = term if total is None else total + term
         return total
 
-    def along(hop):
-        target_row = (row + hop) % slow
+    def along(target_row):
         return remote(
-            sums_ref.at[hop],
+            sums_ref.at[target_row],
             second_ref.at[row],
-            second_send.at[hop],
+            second_send.at[target_row],
             second_recv.at[row],
             target_row * fast + column,
             core,
@@ -293,10 +300,7 @@
     @pl.when(step == 0)
     def _():
         greet(slow, fast)
-        for crossing in crossings():
-            across(*crossing).start()
-        for index in range(near):
-            keep_own(index).start()
+        launch(0)
 
     columns = codes_ref.shape[1]
     totals = [None, None]
@@ -310,12 +314,16 @@
     grad_mine_ref[...] = totals[0].astype(grad_mine_ref.dtype)
     grad_other_ref[...] = totals[1].astype(grad_other_ref.dtype)
 
-    for hop in range(1, slow):
-
-        @pl.when(step == jnp.minimum(last, hop * (last + 1) // (slow - 1)))
+    for wave in range(near):
+
+        @pl.when(step == jnp.minimum(last, (wave + 1) * (last + 1) // (near + 1)))
         def _():
-            sums_ref[hop] = gathered((row + hop) % slow).astype(BF16)
-            along(hop).start()
+            for count, target_row in enumerate(targets(wave)):
+                total = gathered(target_row)
+                sums_ref[target_row] = total.astype(BF16)
+                along(target_row).start()
+                if count == 0 and wave + 1 < near:
+                    launch(wave + 1)
 
     @pl.when(step == last)
     def _():
@@ -326,10 +334,11 @@
             pltpu.make_async_copy(place, place, second_recv.at[source]).wait()
             total = total + second_ref[source].astype(F32)
         rows_ref[...] = total.astype(rows_ref.dtype)
-        for crossing in crossings():
-            across(*crossing).wait_send()
-        for hop in range(1, slow):
-            along(hop).wait_send()
+        for wave in range(near):
+            for copy in crossings(wave):
+                copy.wait_send()
+            for target_row in targets(wave):
+                along(target_row).wait_send()
 
 
 def hidden_grad(cot_all, codes, exponents, out_mine, out_other, slow, fast):

time: 212 us -> 180 us (0.85)
  Pallas kernels: 189 us -> 162 us
  starting transfers between devices: 6.25 us -> 3.12 us
    pallas_call x1, Pallas kernels: 96.2 us -> 68.9 us  [hidden_grad(): pl.pallas_call(functools.partial(hidden_grad_body, tile(columns, 1024), s...]
    ppermute x2, starting transfers between devices: 6.25 us -> 3.12 us  [swap(): return lax.ppermute(value, 'depth', [(0, 1), (1, 0)])]
  transfers between devices with their start and end apart: 2 -> 2, of which waited for: 1 -> 1; matrix products, arithmetic and copies ran while one was open for 0% -> 0% of each run, Pallas kernels for 11% -> 13%
where the time goes in v3:
time: 180 us
  Pallas kernels  162 us (90%)
  other arithmetic  9.5 us (5%)
  waiting for transfers between devices  3.92 us (2%)
  starting transfers between devices  3.12 us (2%)
    pallas_call x1, Pallas kernels, forward(): pl.pallas_call(functools.partial(forward_body, tile(units, 1024), slow, f...  69.7 us
    pallas_call x1, Pallas kernels, hidden_grad(): pl.pallas_call(functools.partial(hidden_grad_body, tile(columns, 1024), s...  68.9 us
    pallas_call x1, Pallas kernels, weight_grad(): pl.pallas_call(functools.partial(weight_grad_body, tile(columns, 1024)),...  23.6 us
    convert_element_type x1, other arithmetic, shards(): grad_up = (grad_hidden * activated).astype(BF16)  5.95 us
    ppermute x2, waiting for transfers between devices, swap(): return lax.ppermute(value, 'depth', [(0, 1), (1, 0)])  3.92 us
  transfers between devices with their start and end apart: 2, of which 1 were waited for; matrix products, arithmetic and copies ran while one was open for 0% of the time, Pallas kernels for 13%

profile of v3, /device:TPU:0, one launch (start us, length us, event | category | flops | bytes accessed | tf_op | source)
XLA Modules:
  0.0 180.2 jit_solution(5581079011131491119)
XLA Ops:
  0.6 3.6 %fusion.mine_ref.h_mine_ref = bf16[256,4096]{1,0:T(8,128)(2,1)S(1)} fusion(bf16[256,4096]{1,0:T(8,128)(2,1)} %param.6, bf16[256,4096]{1,0:T(8,128)(2,1)} %param.5), kind=kLoop, calls=%fused_computation.5 | loop fusion | flops 8388608 | bytes 6291456 | tf_op jit(solution)/shard_map/convert_element_type | solution.py:427
  4.2 0.0 copy-start.1
  4.2 0.5 collective-permute-start
  4.7 3.9 %collective-permute-done.other_ref.h_other_ref = bf16[256,4096]{1,0:T(8,128)(2,1)} collective-permute-done((bf16[256,4096]{1,0:T(8,128)(2,1)S(1)}, bf16[256,4096]{1,0:T(8,128)(2,1)}, u32[]{:S(2)}, u32[]{:S(2)}) %collective-permute-start) | collective-permute-done | bytes 2097184 | tf_op jit(solution)/shard_map/ppermute | solution.py:421
  8.6 0.0 copy-done.1
  8.6 69.7 %forward.1 = (bf16[256,4096]{1,0:T(8,128)(2,1)}, bf16[256,4096]{1,0:T(8,128)(2,1)}, bf16[3,256,4096]{2,1,0:T(8,128)(2,1)}) custom-call(bf16[256,4096]{1,0:T(8,128)(2,1)} %copy-done.1, bf16[256,4096]{1,0:T(8,128)(2,1)} %collective-permute-done.other_ref.h_other_ref, bf16[4096,4096]{1,0:T(8,128)(2,1)} %codes_ref.3, s32[128,4096]{1,0:T(8,128)} %exponents_ref.3, ...), custom_call_target="tpu_custom_call" | custom-call | flops 17179869184 | bytes 33554432 | tf_op jit(solution)/shard_map/forward/pallas_call | solution.py:194
  78.3 68.9 %hidden_grad.1 = (f32[256,4096]{1,0:T(8,128)}, bf16[256,4096]{1,0:T(8,128)(2,1)}, bf16[256,1024]{1,0:T(8,128)(2,1)}) custom-call(bf16[3,256,4096]{2,1,0:T(8,128)(2,1)} %get-tuple-element.10.mine_ref.other_ref.c_mine_ref.c_other_ref, bf16[3,256,4096]{2,1,0:T(8,128)(2,1)} %get-tuple-element.10.mine_ref.other_ref.c_mine_ref.c_other_ref, ...), custom_call_target="tpu_custom_call" | custom-call | flops 17179869184 | bytes 33554432 | tf_op jit(solution)/shard_map/hidden_grad/pallas_call | solution.py:351
  147.2 2.6 %collective-permute-start.1 = (bf16[256,4096]{1,0:T(8,128)(2,1)}, bf16[256,4096]{1,0:T(8,128)(2,1)}, u32[]{:S(2)}, u32[]{:S(2)}) collective-permute-start(bf16[256,4096]{1,0:T(8,128)(2,1)} %get-tuple-element.15), channel_id=1, source_target_pairs={{0,1},{1,0},{2,3},{3,2},{4,5},{5,4},{6,7},{7,6},{8,9},{9,8},{10,11... | collective-permute-start | bytes 6291464 | tf_op jit(solution)/shard_map/ppermute | solution.py:421
  149.8 0.0 copy-start
  149.8 23.6 %weight_grad.1 = bf16[4096,4096]{1,0:T(8,128)(2,1)} custom-call(bf16[256,4096]{1,0:T(8,128)(2,1)} %copy-done.1, bf16[256,4096]{1,0:T(8,128)(2,1)} %collective-permute-done.other_ref.h_other_ref, bf16[3,256,4096]{2,1,0:T(8,128)(2,1)} %get-tuple-element.10.mine_ref.other_ref.c_mine_ref.c_other_ref, ...), custom_call_target="tpu_custom_call" | custom-call | flops 17179869184 | bytes 33554432 | tf_op jit(solution)/shard_map/weight_grad/pallas_call | solution.py:405
  173.4 0.0 collective-permute-done.1
  173.4 0.0 copy-done
  173.4 0.0 copy-start.2
  173.4 5.9 %multiply_convert_fusion = (bf16[256,4096]{1,0:T(8,128)(2,1)}, bf16[256,4096]{1,0:T(8,128)(2,1)}) fusion(f32[256,4096]{1,0:T(8,128)} %get-tuple-element.14, bf16[256,4096]{1,0:T(8,128)(2,1)} %collective-permute-done.1, bf16[256,4096]{1,0:T(8,128)(2,1)} %param.5, bf16[256,4096]{1,0:T(8,128)(2,1)S(1)} %copy-done), kind=kLoop, calls=%fused_computation.13 | loop fusion | flops 17825792 | bytes 14680064 | tf_op jit(solution)/shard_map/convert_element_type | solution.py:440
  179.4 0.0 copy-done.2
  179.4 0.8 copy.10
Async XLA Ops:
  4.2 4.5 %copy-start.1 = (bf16[256,4096]{1,0:T(8,128)(2,1)}, bf16[256,4096]{1,0:T(8,128)(2,1)S(1)}, u32[]{:S(2)}) copy-start(bf16[256,4096]{1,0:T(8,128)(2,1)S(1)} %fusion.mine_ref.h_mine_ref) | copy-start | bytes 6291460
  4.2 4.4 %collective-permute-start = (bf16[256,4096]{1,0:T(8,128)(2,1)S(1)}, bf16[256,4096]{1,0:T(8,128)(2,1)}, u32[]{:S(2)}, u32[]{:S(2)}) collective-permute-start(bf16[256,4096]{1,0:T(8,128)(2,1)S(1)} %fusion.mine_ref.h_mine_ref), channel_id=1, source_target_pairs={{0,1},{1,0},{2,3},{3,2},{4,5},{5,4},{6,7},{7,6},{8,9},{9,8},{10,11... | collective-permute-start | bytes 6291464 | tf_op jit(solution)/shard_map/ppermute | solution.py:421
  147.2 26.2 %collective-permute-start.1 = (bf16[256,4096]{1,0:T(8,128)(2,1)}, bf16[256,4096]{1,0:T(8,128)(2,1)}, u32[]{:S(2)}, u32[]{:S(2)}) collective-permute-start(bf16[256,4096]{1,0:T(8,128)(2,1)} %get-tuple-element.15), channel_id=1, source_target_pairs={{0,1},{1,0},{2,3},{3,2},{4,5},{5,4},{6,7},{7,6},{8,9},{9,8},{10,11... | collective-permute-start | bytes 6291464 | tf_op jit(solution)/shard_map/ppermute | solution.py:421
  149.8 23.6 %copy-start = (bf16[256,4096]{1,0:T(8,128)(2,1)S(1)}, bf16[256,4096]{1,0:T(8,128)(2,1)}, u32[]{:S(2)}) copy-start(bf16[256,4096]{1,0:T(8,128)(2,1)} %param.6) | copy-start | bytes 6291460
  173.4 6.0 %copy-start.2 = (bf16[256,1024]{1,0:T(8,128)(2,1)S(1)}, bf16[256,1024]{1,0:T(8,128)(2,1)}, u32[]{:S(2)}) copy-start(bf16[256,1024]{1,0:T(8,128)(2,1)} %get-tuple-element.22) | copy-start | bytes 1572868
